TPU v7x, 256 devices: a whole 4x4x8 slice. The times are simulated.
256 devices in a mesh: seq: 64 (over z, x, core), head: 4 (over y).
Axes of the slice: x: 4, y: 4, z: 8, core: 2. Of those that a mesh axis runs over, the one named last changes fastest.
Arguments:
- qk: bfloat16 [65536, 2048], P('seq', 'head'), may hold values from -8 to 8
- values: bfloat16 [65536, 2048], P('seq', 'head'), may hold values from -6 to 6
- out_weight: bfloat16 [2048, 2048], P('head'), may hold values from -0.125 to 0.125
- out_cotangent: bfloat16 [65536, 2048], P('seq', 'head'), may hold values from -6 to 6
- cluster_ids: int32 [512, 16], P(None, 'head'), may hold values from 0 to 127, as said below
Outputs:
- output: bfloat16 [65536, 2048], P('seq', 'head')
- grad_qk: bfloat16 [65536, 2048], P('seq', 'head')
- grad_values: bfloat16 [65536, 2048], P('seq', 'head')
Inputs may be any that keep to these rules, and one draw needn't show every extreme that they name: `cluster_ids`: call c // 2 the owner of cluster c. Over the blocks of one seq index and the heads of one head index, at most 2 name clusters of one owner, and exactly 2 for some owner. For every head, the clusters of each owner hold exactly 8 blocks together, and some cluster holds all 8.
All inputs are finite; a program needn't handle non-finite values.
Results may differ from a plain program's by a relative error of at most 0.013.
Values may be sent and summed in bfloat16 or wider, within the bound.
A program may use at most 128 MiB of HBM per device.

v0:
```python
import functools
import math

import jax
import jax.numpy as jnp
import numpy as np
from jax import lax
from jax.experimental import pallas as pl
from jax.experimental.pallas import tpu as pltpu
from jax.sharding import PartitionSpec as P

BLOCK = 128
CL_OWN = 2
N_SEQ = 64
SLABS = 8
CHIPS = 4
ITEMS = 32
POOL = 2 * ITEMS
HD = 4
BLK_DEV = 8
NBLK = 512
TOK = 1024
WIDTH = 512
S1 = 4
I32 = jnp.int32
MESH = pl.DeviceIdType.MESH
NEG = -1e30
LOG2E = math.log2(math.e)
FAST = (5, 15)
FULL = (16, 32)
VMEM_BYTES = 60 * 1024 * 1024


def rng_(n): return jnp.arange(n,dtype=I32)
def pick(hit,value): return jnp.sum(jnp.where(hit,value,0),axis=-1).astype(I32)
def places():
    owner=np.arange(N_SEQ); maps=[]
    for width,mults in ((1,(1,)),(2,(1,3,5,7)),(4,range(1,16,2)),(8,range(1,32,2))):
        for mult in mults:
            e=(mult*owner)%N_SEQ
            maps.append((e//width)%SLABS*8+(e//(width*SLABS))*width+e%width)
    r=np.random.RandomState(7)
    while len(maps)<32: maps.append(r.permutation(N_SEQ))
    return np.stack(maps).astype(np.int32)
PLACES=places()
def choose_places(owners):
    cnt=jnp.sum((owners[:,:,None]==rng_(N_SEQ)).astype(I32),axis=1)
    slab_cnt=jnp.sum(cnt.reshape(SLABS,8,N_SEQ),axis=1)
    n=PLACES.shape[0]
    slab_of=np.zeros((N_SEQ,n*SLABS),np.float32)
    for p in range(n): slab_of[np.arange(N_SEQ),p*SLABS+PLACES[p]//8]=1
    loads=jnp.dot(slab_cnt.astype(jnp.float32),jnp.asarray(slab_of),preferred_element_type=jnp.float32,precision="highest")
    worst=jnp.max(loads.reshape(SLABS,n,SLABS),axis=(0,2))
    best=jnp.argmin(worst).astype(I32)
    return jnp.sum(jnp.where((rng_(n)==best)[:,None],PLACES,0),axis=0)
def routing(me,cluster_ids,place,k2,k3):
    owners=(cluster_ids//CL_OWN).reshape(-1)
    z_me,x_me,c_me=me//8,(me//2)%4,me%2
    cap2,cap3=2*k2,2*k3
    pos=jnp.sum(jnp.where(owners[:,None]==rng_(N_SEQ),place,0),axis=1)
    zc=(pos//8).reshape(SLABS,CHIPS,POOL)
    earlier=rng_(POOL)[None,:]<rng_(POOL)[:,None]
    r=jnp.sum(((zc[...,:,None]==zc[...,None,:])&earlier).astype(I32),axis=-1)
    to=zc[...,None]==rng_(SLABS)
    n=jnp.sum(to.astype(I32),axis=2)
    over,free=jnp.maximum(n-cap2,0),jnp.maximum(cap2-n,0)
    below=(rng_(CHIPS)[None,:]<rng_(CHIPS)[:,None]).astype(I32)
    over_at=jnp.sum(below[None,:,:,None]*over[:,None],axis=2)
    free_at=jnp.sum(below[None,:,:,None]*free[:,None],axis=2)
    extra=r>=cap2
    turn=jnp.sum(jnp.where(to,over_at[:,:,None,:],0),axis=-1)+r-cap2
    def at(v):
        return jnp.sum(jnp.where(to[:,:,:,None,:],v[:,None,None,:,:],0),axis=-1)
    f0=at(free_at)
    hit=extra[...,None]&(f0<=turn[...,None])&(turn[...,None]<f0+at(free))
    own_chip=rng_(CHIPS)[None,:,None]
    via=jnp.where(extra,pick(hit,rng_(CHIPS)),own_chip)
    k=jnp.where(extra,pick(hit,at(n)+turn[...,None]-f0),r)
    s=jnp.sum((extra[...,None,:]&(via[...,:,None]==via[...,None,:])&earlier).astype(I32),axis=-1)
    lost=jnp.any(extra&((s>=2*S1)|~jnp.any(hit,-1)))
    slab_items=CHIPS*POOL
    zf,via,k,s,extra=[v.reshape(SLABS,slab_items) for v in (zc,via,k,s,extra)]
    src=jnp.broadcast_to(own_chip,(SLABS,CHIPS,POOL)).reshape(SLABS,slab_items)
    pos=pos.reshape(SLABS,slab_items)
    xd=(pos//2)%4
    here=zf==z_me
    key=jnp.where(here,via*4+xd,-1)
    before=rng_(slab_items)[None,:]<rng_(slab_items)[:,None]
    w=jnp.sum(((key[:,:,None]==key[:,None,:])&before).astype(I32),axis=-1)
    keyed=key[...,None]==rng_(16)
    hist=jnp.sum(keyed.astype(I32),axis=1)
    upto=(rng_(SLABS)[None,:]<rng_(SLABS)[:,None]).astype(I32)
    base=jnp.sum(upto[:,:,None]*hist[None],axis=1)
    w=w+jnp.sum(jnp.where(keyed,base[:,None,:],0),axis=-1)
    full_key=(zf*CHIPS+via)*CHIPS+xd
    counts=jnp.sum((full_key.reshape(-1,1)==rng_(SLABS*CHIPS*CHIPS)).astype(I32),axis=0)
    lost=lost|(jnp.max(counts)>cap3)
    zslot=zf*k2+k%k2
    rslot=rng_(SLABS)[:,None]*k2+k%k2
    zcore=k//k2
    xslot_out=xd*k3+w%k3
    xslot_in=via*k3+w%k3
    xcore=w//k3
    s_at=(s//S1)*(CHIPS*S1)+s%S1
    row=lambda v: lax.dynamic_index_in_dim(v,z_me,0,keepdims=False)
    R=lambda m: rng_(m)[:,None]
    zf_r,via_r,k_r,s_r,ex_r,src_r,zslot_r,zcore_r,sat_r=[row(v) for v in (zf,via,k,s,extra,src,zslot,zcore,s_at)]
    q=rng_(slab_items)%POOL
    t1=pick(ex_r&(src_r==x_me)&(s_r//S1==c_me)&(via_r*S1+s_r%S1==R(CHIPS*S1)),q)
    t2=pick((via_r==x_me)&(zcore_r==c_me)&(zslot_r==R(SLABS*k2)),jnp.where(ex_r,POOL+sat_r+src_r*S1,q))
    r1=pick(ex_r&(via_r==x_me)&(s_r//S1==c_me)&(src_r*S1+s_r%S1==R(CHIPS*S1)),zcore_r*(SLABS*k2)+zslot_r)
    back=jnp.where(ex_r,2*SLABS*k2+sat_r+via_r*S1,zcore_r*(SLABS*k2)+zslot_r)
    rf=lax.dynamic_slice_in_dim(back,x_me*POOL+c_me*ITEMS,ITEMS,0)
    mid=here&(via==x_me)
    fl=lambda v: v.reshape(-1)
    t3=pick(fl(mid&(xcore==c_me))&(fl(xslot_out)==R(CHIPS*k3)),fl(zcore*(SLABS*k2)+rslot))
    r2=pick((mid&(zcore==c_me))[:,None,:]&((k%k2)[:,None,:]==rng_(k2)[None,:,None]),(xcore*(CHIPS*k3)+xslot_out)[:,None,:]).reshape(-1)
    chip_me=z_me*4+x_me
    heads=lambda v: v.reshape(NBLK,HD).T
    pos_h=heads(pos)
    both=jnp.stack([pos_h==chip_me*2,pos_h==chip_me*2+1])
    upper=jnp.asarray(np.triu(np.ones((NBLK,NBLK)),1),jnp.bfloat16)
    rank=jnp.dot(both.reshape(2*HD,NBLK).astype(jnp.bfloat16),upper,preferred_element_type=jnp.float32).astype(I32).reshape(2,HD,NBLK)
    unit=rank+BLK_DEV*rng_(HD)[None,:,None]+ITEMS*rng_(2)[:,None,None]
    unit=jnp.sum(jnp.where(both,unit,0),axis=0)
    for_chip=both[0]|both[1]
    xin_h,xcore_h=heads(xslot_in),heads(xcore)
    r3=pick((for_chip&(xcore_h==c_me)).reshape(-1)&(xin_h.reshape(-1)==R(CHIPS*k3)),unit.reshape(-1))
    mine=pos_h==me
    slot=mine[:,None,:]&((unit-c_me*ITEMS)[:,None,:]==(rng_(HD)*BLK_DEV)[:,None,None]+rng_(BLK_DEV)[None,:,None])
    tu=pick(slot,(xcore_h*(CHIPS*k3)+xin_h)[:,None,:]).reshape(-1)
    group=pick(slot,cluster_ids.T[:,None,:])
    pad=lambda v,m: jnp.clip(v,0,m)
    P2,P3=2*SLABS*k2,2*CHIPS*k3
    tables=jnp.concatenate([t1,t2,pad(t3,P2-1),pad(tu,P3-1),pad(r3,POOL-1),pad(r2,P3-1),pad(r1,P2-1),pad(rf,P2+2*CHIPS*S1-1)])
    same=group[:,:,None]==group[:,None,:]
    bias=jnp.where(jnp.repeat(same,BLOCK,axis=2),0.0,NEG).astype(jnp.float32)
    return tables,bias,lost


class Link:
    def __init__(self, tab, tasks, inbound, chunks, k2, k3, scratch, sets):
        self.tab, self.k2, self.k3, self.rows = tab, k2, k3, BLOCK // chunks
        self.tasks, self.inbound = tasks, inbound
        self.buf = {t: scratch[7 * (i % sets) : 7 * (i % sets) + 7] for i, t in enumerate(tasks)}
        self.sends, self.recvs = scratch[7 * sets : 7 * sets + 2]
        self.index = {t: i % sets for i, t in enumerate(tasks)}
        self.me = lax.axis_index("seq")
        self.z, self.x, self.c = self.me // 8, (self.me // 2) % CHIPS, self.me % 2
        self.t1, self.t2, self.t3, self.tu, self.r3, self.r2, self.r1, self.rf = table_offsets(k2, k3)[0]
        self.live = {}

    def peer(self, axis, d):
        if axis == "z":
            to = lax.rem(self.z + d, SLABS)
            return to, to * 8 + self.x * 2 + self.c
        if axis == "x":
            to = lax.rem(self.x + d, CHIPS)
            return to, self.z * 8 + to * 2 + self.c
        return 1 - self.c, self.me + 1 - 2 * self.c

    def peers(self):
        out = [self.peer("z", d)[1] for d in range(1, SLABS)]
        out += [self.peer("x", d)[1] for d in range(1, CHIPS)]
        return out + [self.peer("c", 1)[1]]

    def barrier(self, extra=()):
        barrier = pltpu.get_barrier_semaphore()
        peers = self.peers()
        for p in peers:
            pl.semaphore_signal(barrier, inc=1, device_id={"seq": p}, device_id_type=MESH)
        for p in extra:
            pl.semaphore_signal(barrier, inc=1, device_id={"head": p}, device_id_type=MESH)
        pl.semaphore_wait(barrier, len(peers) + len(extra))

    def start(self, task, kind, d, src, dst, peer):
        s = self.index[task] * 7 + kind
        cp = pltpu.make_async_remote_copy(
            src_ref=src,
            dst_ref=dst,
            send_sem=self.sends.at[s, d],
            recv_sem=self.recvs.at[s, d],
            device_id={"seq": peer},
            device_id_type=MESH,
        )
        cp.start()
        self.live.setdefault((task, kind), []).append(cp)

    def share(self, task, kind, ref, half):
        part = ref.at[pl.ds(self.c * half, half)]
        self.start(task, kind, 0, part, part, self.peer("c", 1)[1])

    def wait(self, task, kind):
        for cp in self.live[task, kind]:
            cp.wait_recv()

    def sent(self, task, *kinds):
        for kind in kinds:
            for cp in self.live.pop((task, kind)):
                cp.wait_send()

    def pack(self, task, kind, axis, load, send, recv, count, base):
        n = SLABS if axis == "z" else CHIPS
        order = (4, 3, 5, 2, 6, 1, 7, 0) if axis == "z" else (2, 1, 3, 0)
        mine = self.z if axis == "z" else self.x
        at = self.c * (n * count) + mine * count
        for d in order:
            to, peer = self.peer(axis, d)

            @pl.loop(0, count, unroll=True)
            def _(k):
                tile = load(self.tab[0, base + to * count + k])
                if d == 0:
                    recv[at + k] = tile
                else:
                    send[to * count + k] = tile

            if d:
                self.start(task, kind, d, send.at[pl.ds(to * count, count)], recv.at[pl.ds(at, count)], peer)

    def either(self, first, second, size):
        def load(i):
            a = first[jnp.minimum(i, size - 1)]
            b = second[jnp.maximum(i - size, 0)]
            return jnp.where(i < size, a, b)

        return load

    def run(self, stage, task, src=None, out=None):
        pool, s1, arr, zs, zr, xs, xr = self.buf[task]
        k2, k3, rows = self.k2, self.k3, self.rows
        c = task[1]
        at = slice(c * rows, (c + 1) * rows)
        inward = self.inbound[task[0]]
        if stage == "A":
            if inward:
                for j in range(ITEMS):
                    b, h = j // HD, j % HD
                    pool[self.c * ITEMS + j] = src[
                        b * BLOCK + c * rows : b * BLOCK + (c + 1) * rows, h * BLOCK : (h + 1) * BLOCK
                    ]
            else:

                @pl.loop(0, ITEMS, unroll=8)
                def _(u):
                    pool[self.c * ITEMS + u] = src[u, at, :]

            self.share(task, 0, pool, ITEMS)
        elif stage == "B":
            self.wait(task, 0)
            if inward:
                self.pack(task, 1, "x", lambda i: pool[i], s1, arr, S1, self.t1)
            else:
                self.pack(task, 5, "x", lambda i: pool[i], xs, xr, k3, self.r3)
        elif stage == "C":
            if inward:
                self.wait(task, 1)
                self.share(task, 2, arr, CHIPS * S1)
            else:
                self.wait(task, 5)
                self.share(task, 6, xr, CHIPS * k3)
        elif stage == "D":
            if inward:
                self.wait(task, 2)
                self.sent(task, 0, 1, 2)
                self.pack(task, 3, "z", self.either(pool, arr, POOL), zs, zr, k2, self.t2)
            else:
                self.wait(task, 6)
                self.sent(task, 0, 5, 6)
                self.pack(task, 3, "z", lambda i: xr[i], zs, zr, k2, self.r2)
        elif stage == "E":
            self.wait(task, 3)
            self.share(task, 4, zr, SLABS * k2)
        elif stage == "F":
            self.wait(task, 4)
            self.sent(task, 3, 4)
            if inward:
                self.pack(task, 5, "x", lambda i: zr[i], xs, xr, k3, self.t3)
            else:
                self.pack(task, 1, "x", lambda i: zr[i], s1, arr, S1, self.r1)
        elif stage == "G":
            if inward:
                self.wait(task, 5)
                self.share(task, 6, xr, CHIPS * k3)
            else:
                self.wait(task, 1)
                self.share(task, 2, arr, CHIPS * S1)
        elif stage == "H":
            if inward:
                self.wait(task, 6)
                self.sent(task, 5, 6)

                @pl.loop(0, ITEMS, unroll=8)
                def _(u):
                    out[u, at, :] = xr[self.tab[0, self.tu + u]]
            else:
                self.wait(task, 2)
                self.sent(task, 1, 2)
                load = self.either(zr, arr, 2 * SLABS * k2)

                @pl.loop(0, BLK_DEV)
                def _(b):
                    for h in range(HD):
                        out[pl.ds(pl.multiple_of(b * BLOCK + c * rows, rows), rows), h * BLOCK : (h + 1) * BLOCK] = load(
                            self.tab[0, self.rf + b * HD + h]
                        )


def link_scratch(sets, chunks, k2, k3):
    sizes = (POOL, CHIPS * S1, ITEMS, SLABS * k2, 2 * SLABS * k2, CHIPS * k3, 2 * CHIPS * k3)
    out = []
    for _ in range(sets):
        out += [pltpu.VMEM((s, BLOCK // chunks, BLOCK), jnp.bfloat16) for s in sizes]
    return out + [pltpu.SemaphoreType.DMA((7 * sets, 8))] * 2


def chunked(arrays, chunks):
    return tuple((arr, c) for arr in range(arrays) for c in range(chunks))


def exchange_kernel(inward, caps, tab, src, out, *scratch):
    task = (0, 0)
    link = Link(tab, [task], [inward], 1, *caps, scratch, 1)
    link.barrier()
    for stage in "ABCDEFGH":
        link.run(stage, task, src, out)


def exchange(tables, array, inward, caps, cid):
    vmem = pl.BlockSpec(memory_space=pltpu.VMEM)
    return pl.pallas_call(
        functools.partial(exchange_kernel, inward, caps),
        out_shape=UNITS if inward else TOKENS,
        in_specs=[pl.BlockSpec(memory_space=pltpu.SMEM), vmem],
        out_specs=vmem,
        scratch_shapes=link_scratch(1, 1, *caps),
        compiler_params=pltpu.CompilerParams(
            collective_id=cid, has_side_effects=True, vmem_limit_bytes=VMEM_BYTES
        ),
    )(tables, array)


NT = (((1,), (1,)), ((), ()))
TN = (((0,), (0,)), ((), ()))


def mm(a, b, dims=(((1,), (0,)), ((), ()))):
    return lax.dot_general(a, b, dims, preferred_element_type=jnp.float32)


def diagonal():
    shape = (BLOCK, BLOCK)
    return lax.broadcasted_iota(I32, shape, 0) == lax.broadcasted_iota(I32, shape, 1)


def of_head(ref, h):
    return ref[pl.ds(h * BLK_DEV, BLK_DEV)].reshape(TOK, BLOCK)


def head_forward(h, x_ref, v_ref, bias_ref, att_ref, attt_ref, lse_ref, s_ref, p_ref):
    c2 = (BLOCK ** -0.5) * LOG2E
    x = of_head(x_ref, h)
    diag = diagonal()
    m = jnp.full((1, TOK), NEG, jnp.float32)
    for i in range(BLK_DEV):
        at = slice(i * BLOCK, (i + 1) * BLOCK)
        s_ref[at, :] = mm(x[at, :], x, NT)
        s_ref[at, at] = jnp.where(diag, NEG, s_ref[at, at])
        top = jnp.max(s_ref[at, :], axis=0, keepdims=True)
        m = jnp.maximum(m, top * c2 + bias_ref[h, i : i + 1, :])
    l = jnp.zeros((1, TOK), jnp.float32)
    for i in range(BLK_DEV):
        at = slice(i * BLOCK, (i + 1) * BLOCK)
        p = jnp.exp2(s_ref[at, :] * c2 + (bias_ref[h, i : i + 1, :] - m))
        l = l + jnp.sum(p, axis=0, keepdims=True)
        p_ref[at, :] = p.astype(jnp.bfloat16)
    attt = mm(of_head(v_ref, h), p_ref[...], TN) * (1.0 / l)
    attt_ref[h] = attt
    att_ref[pl.ds(h * BLK_DEV, BLK_DEV)] = attt.T.astype(jnp.bfloat16).reshape(BLK_DEV, BLOCK, BLOCK)
    lse_ref[h] = jnp.broadcast_to(m + jnp.log2(l), (8, TOK))


def head_backward(h, x_ref, v_ref, g_ref, bias_ref, attt_ref, lse_ref, gx_ref, gv_ref, acc_ref, acct_ref):
    c2 = (BLOCK ** -0.5) * LOG2E
    x = of_head(x_ref, h)
    g = of_head(g_ref, h)
    diag = diagonal()
    delta = jnp.sum(g.astype(jnp.float32).T * attt_ref[h], axis=0, keepdims=True)
    lse = lse_ref[h, 0:1, :]
    for i in range(BLK_DEV):
        at = slice(i * BLOCK, (i + 1) * BLOCK)
        x_i = x[at, :]
        p = jnp.exp2(mm(x_i, x, NT) * c2 + (bias_ref[h, i : i + 1, :] - lse))
        own = jnp.where(diag, 0.0, p[:, at])
        parts = [p[:, : i * BLOCK]] * (i > 0) + [own] + [p[:, (i + 1) * BLOCK :]] * (i < BLK_DEV - 1)
        p = jnp.concatenate(parts, axis=1)
        gs = p * (mm(v_ref[h * BLK_DEV + i], g, NT) - delta)
        gv_ref[h * BLK_DEV + i] = mm(p.astype(jnp.bfloat16), g).astype(jnp.bfloat16)
        gsb = gs.astype(jnp.bfloat16)
        acc_ref[at, :] = mm(gsb, x)
        add = mm(x_i, gsb, TN)
        if i == 0:
            acct_ref[...] = add
        else:
            acct_ref[...] += add
    gx = (acc_ref[...] + acct_ref[...].T) * (BLOCK ** -0.5)
    gx_ref[pl.ds(h * BLK_DEV, BLK_DEV)] = gx.astype(jnp.bfloat16).reshape(BLK_DEV, BLOCK, BLOCK)


ROWS_R = 16
PAD = 512


def place_consts():
    n = PLACES.shape[0]
    slab_of = np.zeros((n * SLABS, N_SEQ), np.float32)
    for p in range(n):
        slab_of[p * SLABS + PLACES[p] // 8, np.arange(N_SEQ)] = 1
    pos = np.zeros((N_SEQ, BLOCK), np.float32)
    pos[:, :n] = PLACES.T
    return slab_of, pos


def table_offsets(k2, k3):
    at, out = 0, []
    for size in (CHIPS * S1, SLABS * k2, CHIPS * k3, ITEMS, CHIPS * k3, SLABS * k2, CHIPS * S1, ITEMS):
        out.append(at)
        at += -(-size // 8) * 8
    return out, at


def routing_kernel(caps, me, ids_ref, slab_of_ref, places_ref, tab_ref, bias_ref, flag_ref, pos_ref):
    k2, k3 = caps
    cap2, cap3 = 2 * k2, 2 * k3
    f32, bf16 = jnp.float32, jnp.bfloat16
    if me is None:
        me = lax.axis_index("seq")
    z_me, x_me, c_me = me // 8, (me // 2) % CHIPS, me % 2
    iota = lambda shape, axis: lax.broadcasted_iota(I32, shape, axis)
    item = (ROWS_R, 1, BLOCK)
    row, lane = iota(item, 0), iota(item, 2)
    ids = ids_ref[...]
    owner = ids // CL_OWN
    own_iota = iota((N_SEQ, BLOCK), 0)
    ll = (iota((BLOCK, BLOCK), 0), iota((BLOCK, BLOCK), 1))
    cnt = jnp.zeros((N_SEQ, BLOCK), f32)
    for z in range(SLABS):
        both = (own_iota == owner[2 * z]).astype(f32) + (own_iota == owner[2 * z + 1]).astype(f32)
        cnt += mm(both.astype(bf16), (ll[1] == z).astype(f32).astype(bf16))
    loads = mm(slab_of_ref[...].astype(bf16), cnt.astype(bf16))
    n_place = slab_of_ref.shape[0] // SLABS
    worst = jnp.max(jnp.max(loads.reshape(n_place, SLABS, BLOCK), axis=1), axis=1, keepdims=True)
    best = jnp.min(worst.astype(I32) * 64 + iota((n_place, 1), 0)) % 64
    chosen = jnp.where(iota((N_SEQ, BLOCK), 1) == best, places_ref[...], 0.0)
    place = jnp.sum(chosen, axis=1, keepdims=True)
    for r in range(ROWS_R):
        pos_ref[r] = jnp.sum(jnp.where(own_iota == owner[r], place, 0.0), axis=0, keepdims=True).astype(I32)
    pos = pos_ref[...]
    zc, xd, cd = pos // 8, (pos // 2) % CHIPS, pos % 2
    half = lane // POOL
    x = (row % 2) * 2 + half
    slab = row // 2
    q = lane % POOL
    same_half = (ll[0] // POOL) == (ll[1] // POOL)
    upper = ll[0] < ll[1]
    as_bf = lambda m: m.astype(f32).astype(bf16)

    def times(hot, matrix):
        n = hot.shape[1]
        return mm(hot.reshape(ROWS_R * n, BLOCK).astype(bf16), as_bf(matrix)).astype(I32).reshape(ROWS_R, n, BLOCK)

    def down(hot, value):
        return jnp.sum(jnp.where(hot, value, 0), axis=1, keepdims=True)

    eight = (ROWS_R, 8, BLOCK)
    sub = iota(eight, 1)
    to = sub == zc
    to_f = to.astype(f32)
    rank = times(to_f, same_half & upper)
    first, second = times(to_f, ll[0] < POOL), times(to_f, ll[0] >= POOL)

    def of_slab(v, which):
        v = v.reshape(SLABS, 2, 8, BLOCK)[:, which : which + 1]
        return jnp.concatenate([v, v], axis=1).reshape(eight)

    n = [of_slab(first, 0), of_slab(second, 0), of_slab(first, 1), of_slab(second, 1)]
    over_at = jnp.zeros(eight, I32)
    for m in range(CHIPS):
        over_at += jnp.where(x > m, jnp.maximum(n[m] - cap2, 0), 0)
    turn = over_at + rank - cap2
    extra8 = to & (rank >= cap2)
    via8, k8 = jnp.zeros(eight, I32), jnp.zeros(eight, I32)
    found8 = jnp.zeros(eight, I32)
    free_at = jnp.zeros(eight, I32)
    for m in range(CHIPS):
        free = jnp.maximum(cap2 - n[m], 0)
        hit = extra8 & (turn >= free_at) & (turn < free_at + free)
        via8 = jnp.where(hit, m, via8)
        k8 = jnp.where(hit, n[m] + turn - free_at, k8)
        found8 = jnp.where(hit, 1, found8)
        free_at += free
    extra = down(extra8, 1)
    found = down(extra8, found8)
    via = jnp.where(extra > 0, down(extra8, via8), x)
    k = jnp.where(extra > 0, down(extra8, k8), down(to, rank))
    moved = (extra > 0) & (sub == via)
    s = down(moved, times(moved.astype(f32), same_half & upper))
    here = zc == z_me

    def prefix(hot):
        hot_f = hot.astype(f32)
        inside, total = times(hot_f, upper), times(hot_f, ll[0] >= 0)
        rows, at = [], jnp.zeros(total.shape[1:], I32)
        for r in range(ROWS_R):
            rows.append((inside[r] + at)[None])
            at = at + total[r]
        return down(hot, jnp.concatenate(rows, axis=0))

    w = prefix(here & (iota((ROWS_R, 16, BLOCK), 1) == via * CHIPS + xd))
    for_chip = (pos // 2) == z_me * CHIPS + x_me
    head = lane % HD
    unit = prefix(for_chip & (sub == cd * HD + head)) + head * BLK_DEV + cd * ITEMS
    key = (zc * CHIPS + via) * CHIPS + xd
    counts = jnp.zeros((BLOCK, BLOCK), f32)
    for r in range(ROWS_R):
        counts += (ll[0] == key[r]).astype(f32)
    full = jnp.max(jnp.sum(counts, axis=1, keepdims=True)) > cap3
    bad = jnp.max(jnp.where((extra > 0) & ((s >= 2 * S1) | (found == 0)), 1, 0)) > 0
    flag_ref[...] = jnp.full((8, BLOCK), jnp.where(full | bad, 1.0, 0.0), f32)
    zslot, rslot, zcore = zc * k2 + k % k2, slab * k2 + k % k2, k // k2
    xout, xin, xcore = xd * k3 + w % k3, via * k3 + w % k3, w // k3
    s_at = (s // S1) * (CHIPS * S1) + s % S1
    in_slab = slab == z_me
    is_extra = extra > 0
    zpool = zcore * (SLABS * k2) + zslot
    mid = here & (via == x_me)
    mine = pos == me
    offsets, total = table_offsets(k2, k3)
    p2, p3 = 2 * SLABS * k2, 2 * CHIPS * k3
    entries = [
        (CHIPS * S1, in_slab & is_extra & (x == x_me) & (s // S1 == c_me), via * S1 + s % S1, q),
        (SLABS * k2, in_slab & (via == x_me) & (zcore == c_me), zslot, jnp.where(is_extra, POOL + s_at + x * S1, q)),
        (CHIPS * k3, mid & (xcore == c_me), xout, jnp.minimum(zcore * (SLABS * k2) + rslot, p2 - 1)),
        (ITEMS, mine, unit - c_me * ITEMS, jnp.minimum(xcore * (CHIPS * k3) + xin, p3 - 1)),
        (CHIPS * k3, for_chip & (xcore == c_me), xin, jnp.minimum(unit, POOL - 1)),
        (SLABS * k2, mid & (zcore == c_me), rslot, jnp.minimum(xcore * (CHIPS * k3) + xout, p3 - 1)),
        (CHIPS * S1, in_slab & is_extra & (via == x_me) & (s // S1 == c_me), x * S1 + s % S1, jnp.minimum(zpool, p2 - 1)),
        (
            ITEMS,
            (row == me // 4) & (lane // ITEMS == me % 4),
            lane % ITEMS,
            jnp.minimum(jnp.where(is_extra, p2 + s_at + via * S1, zpool), p2 + ITEMS - 1),
        ),
        (ITEMS, mine, unit - c_me * ITEMS, ids),
    ]
    parts = []
    for size, mask, slot, value in entries:
        size = -(-size // 8) * 8
        target = jnp.where(mask, slot, -1)
        acc = jnp.zeros((size, BLOCK), I32)
        rows = iota((size, BLOCK), 0)
        for r in range(ROWS_R):
            acc += jnp.where(rows == target[r], value[r], 0)
        parts.append(acc.astype(f32))
    group = jnp.sum(parts.pop(), axis=1, keepdims=True)
    parts.append(jnp.zeros((PAD - total, BLOCK), f32))
    everything = jnp.concatenate(parts, axis=0).astype(bf16)
    tab_ref[...] = mm(jnp.ones((8, BLOCK), bf16), everything, NT).astype(I32)
    for h in range(HD):
        rows = group[h * BLK_DEV : (h + 1) * BLK_DEV]
        for j in range(BLK_DEV):
            one = group[h * BLK_DEV + j : h * BLK_DEV + j + 1]
            tile = jnp.where(jnp.broadcast_to(rows, (BLK_DEV, BLOCK)) == jnp.broadcast_to(one, (BLK_DEV, BLOCK)), 0.0, NEG)
            bias_ref[h, :, j * BLOCK : (j + 1) * BLOCK] = tile


def fast_routing(cluster_ids, caps, me=None, interpret=False):
    slab_of, pos = place_consts()
    vmem = pl.BlockSpec(memory_space=pltpu.VMEM)
    return pl.pallas_call(
        functools.partial(routing_kernel, caps, me),
        out_shape=[
            jax.ShapeDtypeStruct((8, PAD), I32),
            jax.ShapeDtypeStruct((HD, BLK_DEV, TOK), jnp.float32),
            jax.ShapeDtypeStruct((8, BLOCK), jnp.float32),
        ],
        in_specs=[vmem] * 3,
        out_specs=[vmem] * 3,
        scratch_shapes=[pltpu.VMEM((ROWS_R, 1, BLOCK), I32)],
        interpret=interpret,
    )(cluster_ids.reshape(ROWS_R, 1, BLOCK), jnp.asarray(slab_of), jnp.asarray(pos))


FORWARD_SCRATCH = (
    pltpu.VMEM((HD, BLOCK, TOK), jnp.float32),
    pltpu.VMEM((HD, 8, TOK), jnp.float32),
    pltpu.VMEM((TOK, TOK), jnp.float32),
    pltpu.VMEM((TOK, TOK), jnp.bfloat16),
)
BACKWARD_SCRATCH = (pltpu.VMEM((TOK, BLOCK), jnp.float32), pltpu.VMEM((BLOCK, TOK), jnp.float32))
UNITS = jax.ShapeDtypeStruct((ITEMS, BLOCK, BLOCK), jnp.bfloat16)
TOKENS = jax.ShapeDtypeStruct((TOK, WIDTH), jnp.bfloat16)


CHUNKS = 4
SETS = 8
ROWS = 256


class Heads:
    def __init__(self, sems):
        self.y = lax.axis_index("head")
        self.others = [lax.rem(self.y + d, 4) for d in range(1, 4)]
        self.sends, self.recvs = sems

    def copy(self, kind, d, src, dst):
        return pltpu.make_async_remote_copy(
            src_ref=src,
            dst_ref=dst,
            send_sem=self.sends.at[kind, d],
            recv_sem=self.recvs.at[kind, d],
            device_id={"head": self.others[d]},
            device_id_type=MESH,
        )

    def columns(self, y):
        return pl.ds(pl.multiple_of(y * WIDTH, WIDTH), WIDTH)


def layer_kernel(caps, tab, flag, qk, values, cot, weight, bias, output, grad_qk, grad_values, any_flag, *scratch):
    scratch = list(scratch)
    attt, lse, s_ref, p_ref, acc, acct = scratch[:6]
    x_u, v_u, g_u, att_u, gv_u, tokens, parts_in, parts_out, flags = scratch[6:15]
    heads = Heads(scratch[15:17])
    ready = scratch[17]
    gx_u = att_u
    tasks = chunked(6, CHUNKS)
    link = Link(tab, tasks, [True] * 3 + [False] * 3, CHUNKS, *caps, scratch[18:], SETS)
    srcs = (qk, values, tokens, att_u, gx_u, gv_u)
    outs = (x_u, v_u, g_u, tokens, grad_qk, grad_values)
    link.barrier(heads.others)

    def step(stages, *which):
        for i in which:
            for stage in stages:
                if 0 <= i < len(tasks):
                    arr = tasks[i][0]
                    link.run(stage, tasks[i], srcs[arr], outs[arr])

    def each(stage, which):
        for i in which:
            step(stage, i)

    flags[heads.y] = flag[...]
    flag_cps = [heads.copy(0, d, flag, flags.at[heads.y]) for d in range(3)]
    cot_cps = [heads.copy(1, d, cot, parts_in.at[heads.y]) for d in range(3)]

    def tick(t):
        step("H", t - 2)
        step("E", t)
        if t + 2 < 8:
            step("D", t + 2)
        if t + 3 < 8:
            step("C", t + 3)
        if t + 4 < 8:
            step("B", t + 4)
        if t + 5 < 8:
            step("A", t + 5)
        step("F", t)
        step("G", t - 1)

    tick(-5)
    for cp in flag_cps + [cot_cps[1], cot_cps[0], cot_cps[2]]:
        cp.start()
    for t in range(-4, 7):
        tick(t)

    for cp in cot_cps:
        cp.wait()

    @pl.loop(0, TOK // ROWS)
    def _(r):
        at = pl.ds(pl.multiple_of(r * ROWS, ROWS), ROWS)
        total = mm(cot[at, :], weight[:, heads.columns(heads.y)], NT)
        for other in heads.others:
            total += mm(parts_in[other, at, :], weight[:, heads.columns(other)], NT)
        tokens[at, :] = total.astype(jnp.bfloat16)

    for other in heads.others:
        pl.semaphore_signal(ready, inc=1, device_id={"head": other}, device_id_type=MESH)

    each("A", range(8, 12))
    each("B", range(8, 12))
    step("CD", 8)
    step("H", 5)
    step("E", 7)
    step("CD", 9)
    step("F", 7)
    step("G", 6)
    step("CD", 10)
    step("H", 6)
    step("E", 8)
    step("CD", 11)
    step("F", 8)
    step("G", 7)
    step("H", 7)
    step("E", 9)
    step("F", 9)
    step("G", 8)

    @pl.loop(0, HD)
    def _(h):
        head_forward(h, x_u, v_u, bias, att_u, attt, lse, s_ref, p_ref)

    each("A", range(12, 16))
    each("B", range(12, 15))
    step("H", 8)
    step("E", 10)
    step("CD", 12)
    step("F", 10)
    step("G", 9)
    step("B", 15)
    step("CD", 13)
    step("H", 9)
    step("E", 11)
    step("CD", 14)
    step("F", 11)
    step("G", 10)
    step("CD", 15)
    step("H", 10)
    step("E", 12)
    step("G", 11)
    step("F", 12)
    step("H", 11)
    step("E", 13)
    step("F", 13)
    step("G", 12)

    @pl.loop(0, HD)
    def _(h):
        head_backward(h, x_u, v_u, g_u, bias, attt, lse, gx_u, gv_u, acc, acct)

    each("A", range(16, 20))
    step("G", 13)
    each("B", range(16, 20))
    step("H", 12)
    step("E", 14)
    step("CD", 16)
    step("F", 14)
    step("CD", 17)
    step("H", 13)
    step("E", 15)
    step("CD", 18)
    step("F", 15)
    step("G", 14)
    step("CD", 19)
    step("A", 20)
    sums = [heads.copy(2, d, parts_out.at[d], parts_in.at[heads.y]) for d in range(3)]
    for t in range(16, 26):
        step("H", t - 2)
        step("E", t)
        step("D", t + 2 if t >= 18 else -1)
        step("C", t + 3 if t >= 17 else -1)
        step("B", t + 4)
        step("A", t + 5)
        step("F", t)
        step("G", t - 1)
        if t == 17:
            pl.semaphore_wait(ready, 3)
            for d in (1, 0, 2):

                @pl.loop(0, TOK // ROWS)
                def _(r):
                    at = pl.ds(pl.multiple_of(r * ROWS, ROWS), ROWS)
                    part = mm(tokens[at, :], weight[:, heads.columns(heads.others[d])])
                    parts_out[d, at, :] = part.astype(jnp.bfloat16)

                sums[d].start()

            @pl.loop(0, TOK // ROWS)
            def _(r):
                at = pl.ds(pl.multiple_of(r * ROWS, ROWS), ROWS)
                output[at, :] = mm(tokens[at, :], weight[:, heads.columns(heads.y)]).astype(jnp.bfloat16)

    for cp in flag_cps + sums:
        cp.wait()
    any_flag[...] = jnp.max(flags[...], axis=0)

    @pl.loop(0, TOK // ROWS)
    def _(r):
        at = pl.ds(pl.multiple_of(r * ROWS, ROWS), ROWS)
        total = output[at, :].astype(jnp.float32)
        for other in heads.others:
            total += parts_in[other, at, :].astype(jnp.float32)
        output[at, :] = total.astype(jnp.bfloat16)


def layer(tables, flag, qk, values, cot, weight, bias, caps, cid):
    vmem = pl.BlockSpec(memory_space=pltpu.VMEM)
    units = pltpu.VMEM((ITEMS, BLOCK, BLOCK), jnp.bfloat16)
    tokens = pltpu.VMEM((TOK, WIDTH), jnp.bfloat16)
    scratch = list(FORWARD_SCRATCH + BACKWARD_SCRATCH) + [units] * 5 + [tokens]
    scratch += [
        pltpu.VMEM((4, TOK, WIDTH), jnp.bfloat16),
        pltpu.VMEM((3, TOK, WIDTH), jnp.bfloat16),
        pltpu.VMEM((4, 8, BLOCK), jnp.float32),
        pltpu.SemaphoreType.DMA((3, 3)),
        pltpu.SemaphoreType.DMA((3, 3)),
        pltpu.SemaphoreType.REGULAR,
    ]
    return pl.pallas_call(
        functools.partial(layer_kernel, caps),
        out_shape=[TOKENS] * 3 + [jax.ShapeDtypeStruct((8, BLOCK), jnp.float32)],
        in_specs=[pl.BlockSpec(memory_space=pltpu.SMEM)] + [vmem] * 6,
        out_specs=[vmem] * 4,
        scratch_shapes=scratch + link_scratch(SETS, CHUNKS, *caps),
        compiler_params=pltpu.CompilerParams(
            collective_id=cid, has_side_effects=True, vmem_limit_bytes=VMEM_BYTES
        ),
    )(tables, flag, qk, values, cot, weight, bias)


def attention_kernel(x_ref, v_ref, g_ref, bias_ref, att, gx_ref, gv_ref, attt, lse, s_ref, p_ref, acc, acct):
    @pl.loop(0, HD)
    def _(h):
        head_forward(h, x_ref, v_ref, bias_ref, att, attt, lse, s_ref, p_ref)
        head_backward(h, x_ref, v_ref, g_ref, bias_ref, attt, lse, gx_ref, gv_ref, acc, acct)


def attention(x, v, g, bias):
    vmem = pl.BlockSpec(memory_space=pltpu.VMEM)
    return pl.pallas_call(
        attention_kernel,
        out_shape=[UNITS] * 3,
        in_specs=[vmem] * 4,
        out_specs=[vmem] * 3,
        scratch_shapes=list(FORWARD_SCRATCH + BACKWARD_SCRATCH),
        compiler_params=pltpu.CompilerParams(vmem_limit_bytes=VMEM_BYTES),
    )(x, v, g, bias)


def model_output(attended, out_weight):
    partial_term = jnp.dot(attended, out_weight, preferred_element_type=jnp.float32)
    return lax.psum_scatter(partial_term.astype(jnp.bfloat16), "head", scatter_dimension=1, tiled=True)


def cotangent_heads(out_cotangent, out_weight):
    gathered = lax.all_gather(out_cotangent, "head", axis=1, tiled=True)
    return jnp.einsum("tn,kn->tk", gathered, out_weight, preferred_element_type=jnp.float32).astype(
        jnp.bfloat16
    )


def per_device(qk, values, out_weight, out_cotangent, cluster_ids):
    tables, bias, flag = fast_routing(cluster_ids, FAST)
    *fast, any_lost = layer(tables, flag, qk, values, out_cotangent, out_weight, bias, FAST, 0)

    def slow(args):
        me = lax.axis_index("seq").astype(I32)
        place = choose_places((cluster_ids // CL_OWN).reshape(N_SEQ, ITEMS))
        tables, bias, _ = routing(me, cluster_ids, place, *FULL)
        tables = tables[None]
        grad_attended = cotangent_heads(out_cotangent, out_weight)
        sources = jnp.stack([qk, values, grad_attended])
        x, v, g = lax.map(lambda a: exchange(tables, a, True, FULL, 1), sources)
        units = jnp.stack(attention(x, v, g, bias))
        home = lax.map(lambda a: exchange(tables, a, False, FULL, 2), units)
        return [model_output(home[0], out_weight), home[1], home[2]]

    return tuple(lax.cond(any_lost[0, 0] > 0, slow, lambda args: args, fast))


def solution(mesh):
    return jax.shard_map(
        per_device,
        mesh=mesh,
        in_specs=(
            P("seq", "head"),
            P("seq", "head"),
            P("head", None),
            P("seq", "head"),
            P(None, "head"),
        ),
        out_specs=(P("seq", "head"), P("seq", "head"), P("seq", "head")),
        check_vma=False,
    )
```

profile of v0, /device:TPU:1, one launch (start us, length us, event | category | flops | bytes accessed | tf_op | source)
XLA Modules:
  0.0 290.0 jit_solution(8296507880604144364)
XLA Ops:
  7.2 0.0 copy-start.6
  7.2 0.0 copy-start.2
  7.2 1.0 copy.135
  8.2 0.8 reshape.714
  8.9 3.8 %shard_map.130 = (s32[8,512]{1,0:T(8,128)}, f32[4,8,1024]{2,1,0:T(8,128)}, f32[8,128]{1,0:T(8,128)}) custom-call(s32[16,1,128]{2,1,0:T(1,128)} %bitcast.112, f32[256,64]{1,0:T(8,128)} %constant.288.clone.slab_of_ref, f32[64,128]{1,0:T(8,128)} %constant.289.clone.places_ref), custom_call_target="tpu_custom_call" | custom-call | tf_op jit(solution)/shard_map/pallas_call | solution.py:580
  12.8 262.6 %shard_map.131 = (bf16[1024,512]{1,0:T(8,128)(2,1)}, bf16[1024,512]{1,0:T(8,128)(2,1)}, bf16[1024,512]{1,0:T(8,128)(2,1)}, f32[8,128]{1,0:T(8,128)}) custom-call(s32[8,512]{1,0:T(8,128)} %get-tuple-element.88.tab, f32[8,128]{1,0:T(8,128)} %get-tuple-element.89.flag, bf16[1024,512]{1,0:T(8,128)(2,1)} %qk.1, bf16[1024,512]{1,0:T(8,128)(2,1)} %values.1, ...), custom_call_target="tpu_custom_call" | custom-call | tf_op jit(solution)/shard_map/pallas_call | solution.py:811
  275.4 1.2 slice.12
  277.2 0.0 copy-done.6
  277.2 0.0 copy-done.2
  277.2 0.3 conditional.1
  277.6 0.0 copy-start.5
  277.6 2.4 copy.174
  279.9 2.3 copy.175
  282.2 0.0 copy-done.5
  282.2 1.0 copy.176
Async XLA Ops:
  7.2 270.1 %copy-start.6 = (s32[512,4]{0,1:T(4,128)S(1)}, s32[512,4]{0,1:T(4,128)}, u32[]{:S(2)}) copy-start(s32[512,4]{0,1:T(4,128)} %param.20) | copy-start | bytes 24580
  7.2 270.1 %copy-start.2 = (bf16[512,2048]{1,0:T(8,128)(2,1)S(1)}, bf16[512,2048]{1,0:T(8,128)(2,1)}, u32[]{:S(2)}) copy-start(bf16[512,2048]{1,0:T(8,128)(2,1)} %weight.1) | copy-start | bytes 6291460
  277.6 4.6 %copy-start.5 = (bf16[1024,512]{1,0:T(8,128)(2,1)S(1)}, bf16[1024,512]{1,0:T(8,128)(2,1)}, u32[]{:S(2)}) copy-start(bf16[1024,512]{1,0:T(8,128)(2,1)} %get-tuple-element.319) | copy-start | bytes 3145732
where the time goes:
time: 290 us
  Pallas kernels  266 us (92%)
  between operations  14.7 us (5%)
  local copies, waits for them, and re-layouts  8.53 us (3%)
    pallas_call x1, Pallas kernels, layer(): pl.pallas_call(functools.partial(layer_kernel, caps), out_shape=[TOKENS]...  263 us
    unnamed x10, local copies, waits for them, and re-layouts  6.58 us

commit v1 on v0

--- a/solution.py
+++ b/solution.py
@@ -695,63 +695,65 @@
     step("H", 5)
     step("E", 7)
     step("CD", 9)
+    step("G", 6)
+    step("H", 6)
     step("F", 7)
-    step("G", 6)
     step("CD", 10)
-    step("H", 6)
-    step("E", 8)
     step("CD", 11)
-    step("F", 8)
     step("G", 7)
     step("H", 7)
+
+    @pl.loop(0, HD)
+    def _(h):
+        head_forward(h, x_u, v_u, bias, att_u, attt, lse, s_ref, p_ref)
+
+    each("A", range(12, 16))
+    each("B", range(12, 15))
+    step("E", 8)
+    step("F", 8)
+    step("C", 12)
+    step("B", 15)
+    step("D", 12)
     step("E", 9)
     step("F", 9)
     step("G", 8)
-
-    @pl.loop(0, HD)
-    def _(h):
-        head_forward(h, x_u, v_u, bias, att_u, attt, lse, s_ref, p_ref)
-
-    each("A", range(12, 16))
-    each("B", range(12, 15))
+    step("CD", 13)
     step("H", 8)
     step("E", 10)
-    step("CD", 12)
     step("F", 10)
     step("G", 9)
-    step("B", 15)
-    step("CD", 13)
+    step("CD", 14)
     step("H", 9)
     step("E", 11)
-    step("CD", 14)
     step("F", 11)
     step("G", 10)
     step("CD", 15)
     step("H", 10)
+    step("G", 11)
+    step("H", 11)
+
+    @pl.loop(0, HD)
+    def _(h):
+        head_backward(h, x_u, v_u, g_u, bias, attt, lse, gx_u, gv_u, acc, acct)
+
+    each("A", range(16, 20))
+    each("B", range(16, 18))
     step("E", 12)
-    step("G", 11)
     step("F", 12)
-    step("H", 11)
     step("E", 13)
     step("F", 13)
     step("G", 12)
-
-    @pl.loop(0, HD)
-    def _(h):
-        head_backward(h, x_u, v_u, g_u, bias, attt, lse, gx_u, gv_u, acc, acct)
-
-    each("A", range(16, 20))
-    step("G", 13)
-    each("B", range(16, 20))
+    each("B", range(18, 20))
+    step("CD", 16)
     step("H", 12)
     step("E", 14)
-    step("CD", 16)
     step("F", 14)
+    step("G", 13)
     step("CD", 17)
     step("H", 13)
     step("E", 15)
+    step("F", 15)
     step("CD", 18)
-    step("F", 15)
     step("G", 14)
     step("CD", 19)
     step("A", 20)

time: 290 us -> 296 us (1.021)
  Pallas kernels: 266 us -> 272 us
    pallas_call x1, Pallas kernels: 263 us -> 268 us  [layer(): pl.pallas_call(functools.partial(layer_kernel, caps), out_shape=[TOKENS]...]
where the time goes in v1:
time: 296 us
  Pallas kernels  272 us (92%)
  between operations  14.7 us (5%)
  local copies, waits for them, and re-layouts  8.53 us (3%)
    pallas_call x1, Pallas kernels, layer(): pl.pallas_call(functools.partial(layer_kernel, caps), out_shape=[TOKENS]...  268 us
    unnamed x10, local copies, waits for them, and re-layouts  6.58 us

profile of v1, /device:TPU:1, one launch (start us, length us, event | category | flops | bytes accessed | tf_op | source)
XLA Modules:
  0.0 295.9 jit_solution(13382323085332836842)
XLA Ops:
  7.2 0.0 copy-start.6
  7.2 0.0 copy-start.2
  7.2 1.0 copy.135
  8.2 0.8 reshape.714
  8.9 3.8 %shard_map.130 = (s32[8,512]{1,0:T(8,128)}, f32[4,8,1024]{2,1,0:T(8,128)}, f32[8,128]{1,0:T(8,128)}) custom-call(s32[16,1,128]{2,1,0:T(1,128)} %bitcast.112, f32[256,64]{1,0:T(8,128)} %constant.288.clone.slab_of_ref, f32[64,128]{1,0:T(8,128)} %constant.289.clone.places_ref), custom_call_target="tpu_custom_call" | custom-call | tf_op jit(solution)/shard_map/pallas_call | solution.py:580
  12.8 268.5 %shard_map.131 = (bf16[1024,512]{1,0:T(8,128)(2,1)}, bf16[1024,512]{1,0:T(8,128)(2,1)}, bf16[1024,512]{1,0:T(8,128)(2,1)}, f32[8,128]{1,0:T(8,128)}) custom-call(s32[8,512]{1,0:T(8,128)} %get-tuple-element.88.tab, f32[8,128]{1,0:T(8,128)} %get-tuple-element.89.flag, bf16[1024,512]{1,0:T(8,128)(2,1)} %qk.1, bf16[1024,512]{1,0:T(8,128)(2,1)} %values.1, ...), custom_call_target="tpu_custom_call" | custom-call | tf_op jit(solution)/shard_map/pallas_call | solution.py:813
  281.3 1.2 slice.12
  283.1 0.0 copy-done.6
  283.1 0.0 copy-done.2
  283.1 0.3 conditional.1
  283.4 0.0 copy-start.5
  283.5 2.4 copy.174
  285.8 2.3 copy.175
  288.1 0.0 copy-done.5
  288.1 1.0 copy.176
Async XLA Ops:
  7.2 276.0 %copy-start.6 = (s32[512,4]{0,1:T(4,128)S(1)}, s32[512,4]{0,1:T(4,128)}, u32[]{:S(2)}) copy-start(s32[512,4]{0,1:T(4,128)} %param.20) | copy-start | bytes 24580
  7.2 276.0 %copy-start.2 = (bf16[512,2048]{1,0:T(8,128)(2,1)S(1)}, bf16[512,2048]{1,0:T(8,128)(2,1)}, u32[]{:S(2)}) copy-start(bf16[512,2048]{1,0:T(8,128)(2,1)} %weight.1) | copy-start | bytes 6291460
  283.4 4.6 %copy-start.5 = (bf16[1024,512]{1,0:T(8,128)(2,1)S(1)}, bf16[1024,512]{1,0:T(8,128)(2,1)}, u32[]{:S(2)}) copy-start(bf16[1024,512]{1,0:T(8,128)(2,1)} %get-tuple-element.319) | copy-start | bytes 3145732
